TPU v7x, 32 devices: a whole 2x2x4 slice. The times are simulated.
32 devices in a mesh: shard: 4 (over y, x), ctx: 2 (over core), tp: 4 (over z).
Axes of the slice: x: 2, y: 2, z: 4, core: 2. Of those that a mesh axis runs over, the one named last changes fastest.
Arguments:
- activations: bfloat16 [4, 2048, 1024], P('shard', 'ctx'), may hold values from -6 to 6
- timestep: int32 [4], P('shard'), may hold values from 0 to 999
- positions: int32 [4, 2048], P('shard', 'ctx'), may hold values from 0 to 16383
- qkv_weight: bfloat16 [3, 1024, 1024], P(None, 'shard', 'tp'), may hold values from -0.1875 to 0.1875
- out_weight: bfloat16 [1024, 1024], P('tp', 'shard'), may hold values from -4 to 4
- up_weight: bfloat16 [1024, 4096], P('shard', 'tp'), may hold values from -0.1875 to 0.1875
- down_weight: bfloat16 [4096, 1024], P('tp', 'shard'), may hold values from -0.125 to 0.125
- time_weight: bfloat16 [256, 4, 1024], P(None, None, 'shard'), may hold values from -0.1875 to 0.1875
- norm_gains: bfloat16 [2, 1024], P(None, 'shard'), may hold values from 0.5 to 1.5
- cotangent: bfloat16 [4, 2048, 1024], P('shard', 'ctx'), may hold values from -6 to 6
Outputs:
- output: bfloat16 [4, 2048, 1024], P('shard', 'ctx')
- input_grad: bfloat16 [4, 2048, 1024], P('shard', 'ctx')
- grad_qkv: float32 [3, 1024, 1024], P(None, 'shard', 'tp')
- grad_out: float32 [1024, 1024], P('tp', 'shard')
- grad_up: float32 [1024, 4096], P('shard', 'tp')
- grad_down: float32 [4096, 1024], P('tp', 'shard')
- grad_time: float32 [256, 4, 1024], P(None, None, 'shard')
- grad_gains: float32 [2, 1024], P(None, 'shard')
All inputs are finite; a program needn't handle non-finite values.
Results may differ from a plain program's by a relative error of at most 0.015.
Values may be sent and summed in bfloat16 or wider, within the bound.
No kernel may reach another device: no remote copies, remote signals or barrier semaphores. Data moves between devices by JAX's collectives and lax.ppermute only.
A program may use at most 320 MiB of HBM per device.

v0:
```python
from functools import partial
import math
import jax
import jax.numpy as jnp
from jax import lax
from jax.sharding import PartitionSpec as P

HEAD_DIM = 64
TEMB = 256
highest = lax.Precision.HIGHEST
norm_epsilon = 1e-05


def embed_time(timestep):
    half_width = TEMB // 2
    frequency = jnp.exp(-math.log(10000.0) * jnp.arange(half_width, dtype=jnp.float32) / half_width)
    angles = timestep.astype(jnp.float32)[:, None] * frequency[None, :]
    return jnp.concatenate([jnp.sin(angles), jnp.cos(angles)], axis=-1)


def rotary_tables(positions):
    half_width = HEAD_DIM // 2
    frequency = jnp.exp(-math.log(10000.0) * jnp.arange(half_width, dtype=jnp.float32) / half_width)
    angles = positions.astype(jnp.float32)[..., None] * frequency
    return (jnp.cos(angles), jnp.sin(angles))


def rotate(heads_in, cosines, sines):
    half_width = HEAD_DIM // 2
    first = heads_in[..., :half_width]
    second = heads_in[..., half_width:]
    cos_wide = cosines[..., None, :]
    sin_wide = sines[..., None, :]
    return jnp.concatenate(
        [first * cos_wide - second * sin_wide, second * cos_wide + first * sin_wide], axis=-1
    )


def unrotate(heads_in, cosines, sines):
    half_width = HEAD_DIM // 2
    first = heads_in[..., :half_width]
    second = heads_in[..., half_width:]
    cos_wide = cosines[..., None, :]
    sin_wide = sines[..., None, :]
    return jnp.concatenate(
        [first * cos_wide + second * sin_wide, second * cos_wide - first * sin_wide], axis=-1
    )


def scaled_norm(values, gain_vec, scaling, offset):
    centered = values - jnp.mean(values, axis=-1, keepdims=True)
    variance = jnp.mean(centered * centered, axis=-1, keepdims=True)
    inverse_std = lax.rsqrt(variance + norm_epsilon)
    normed = centered * inverse_std
    return (
        normed * gain_vec * (1.0 + scaling[:, None, :]) + offset[:, None, :],
        normed,
        inverse_std,
    )


def norm_back(grad_in, normed, inverse_std, gain_vec, scaling):
    factor = gain_vec * (1.0 + scaling[:, None, :])
    grad_normed = grad_in * factor
    grad_values = inverse_std * (
        grad_normed
        - jnp.mean(grad_normed, axis=-1, keepdims=True)
        - normed * jnp.mean(grad_normed * normed, axis=-1, keepdims=True)
    )
    grad_gain = jnp.sum(grad_in * normed * (1.0 + scaling[:, None, :]), axis=(0, 1))
    grad_scaling = jnp.sum(grad_in * normed * gain_vec, axis=1)
    grad_offset = jnp.sum(grad_in, axis=1)
    return (grad_values, grad_gain, grad_scaling, grad_offset)


def group_heads(field, per_group):
    seq_count, rows_count, _ = field.shape
    split = field.reshape(seq_count, rows_count, -1, HEAD_DIM).transpose(0, 2, 1, 3)
    return split.reshape(-1, per_group, rows_count, HEAD_DIM)


def ungroup_heads(field, seq_count):
    rows_count = field.shape[2]
    joined = field.reshape(seq_count, -1, rows_count, HEAD_DIM).transpose(0, 2, 1, 3)
    return joined.reshape(seq_count, rows_count, -1)


def attend_block(triple, scaling):
    queries, keys, values = triple
    scores = jnp.einsum("gqd,gkd->gqk", queries, keys, preferred_element_type=jnp.float32) * scaling
    top_score = jnp.max(scores, axis=-1, keepdims=True)
    raised = jnp.exp(scores - top_score)
    total = jnp.sum(raised, axis=-1, keepdims=True)
    weights = (raised / total).astype(jnp.bfloat16)
    attended = jnp.einsum("gqk,gkd->gqd", weights, values, preferred_element_type=jnp.float32)
    return (attended, (top_score + jnp.log(total))[..., 0])


def attend_back(bundle, scaling):
    queries, keys, values, grad_out, log_total = bundle
    scores = jnp.einsum("gqd,gkd->gqk", queries, keys, preferred_element_type=jnp.float32) * scaling
    weights = jnp.exp(scores - log_total[..., None])
    grad_values = jnp.einsum(
        "gqk,gqd->gkd", weights.astype(jnp.bfloat16), grad_out, preferred_element_type=jnp.float32
    )
    grad_weights = jnp.einsum("gqd,gkd->gqk", grad_out, values, preferred_element_type=jnp.float32)
    row_term = jnp.sum(weights * grad_weights, axis=-1, keepdims=True)
    grad_scores = (weights * (grad_weights - row_term)).astype(jnp.bfloat16)
    grad_queries = (
        jnp.einsum("gqk,gkd->gqd", grad_scores, keys, preferred_element_type=jnp.float32) * scaling
    )
    grad_keys = (
        jnp.einsum("gqk,gqd->gkd", grad_scores, queries, preferred_element_type=jnp.float32)
        * scaling
    )
    return (grad_queries, grad_keys, grad_values)


def gelu_slope(hidden):
    return (
        0.5 * (1.0 + lax.erf(hidden * 0.7071067811865476))
        + hidden * jnp.exp(-0.5 * hidden * hidden) * 0.3989422804014327
    )


def body(
    activations,
    timestep,
    positions,
    qkv_weight,
    out_weight,
    up_weight,
    down_weight,
    time_weight,
    norm_gains,
    cotangent,
):
    seq_count, tokens, width = activations.shape
    local_width = qkv_weight.shape[2]
    heads_local = local_width // HEAD_DIM
    per_group = min(heads_local, max(1, 512 // tokens))
    while heads_local % per_group:
        per_group -= 1
    scaling = HEAD_DIM ** (-0.5)
    full_qkv, full_out, full_up, full_down, full_time, full_gains = (
        lax.all_gather(qkv_weight, "shard", axis=1, tiled=True),
        lax.all_gather(out_weight, "shard", axis=1, tiled=True),
        lax.all_gather(up_weight, "shard", axis=0, tiled=True),
        lax.all_gather(down_weight, "shard", axis=1, tiled=True),
        lax.all_gather(time_weight, "shard", axis=2, tiled=True),
        lax.all_gather(norm_gains, "shard", axis=1, tiled=True),
    )
    gains_f = full_gains.astype(jnp.float32)
    embedding = embed_time(timestep)
    modulation = jnp.einsum(
        "sk,kcd->scd", embedding, full_time.astype(jnp.float32), precision=highest
    )
    cosines, sines = rotary_tables(positions)
    inputs_f = activations.astype(jnp.float32)
    first_out, normed_one, inverse_one = scaled_norm(
        inputs_f, gains_f[0], modulation[:, 0], modulation[:, 1]
    )
    first_low = first_out.astype(jnp.bfloat16)
    projected = jnp.einsum("std,cde->cste", first_low, full_qkv, preferred_element_type=jnp.float32)
    head_shape = (seq_count, tokens, heads_local, HEAD_DIM)
    query_rot = (
        rotate(projected[0].reshape(head_shape), cosines, sines)
        .reshape(seq_count, tokens, local_width)
        .astype(jnp.bfloat16)
    )
    key_rot = (
        rotate(projected[1].reshape(head_shape), cosines, sines)
        .reshape(seq_count, tokens, local_width)
        .astype(jnp.bfloat16)
    )
    value_low = projected[2].astype(jnp.bfloat16)
    keys_all, values_all = (
        lax.all_gather(key_rot, "ctx", axis=1, tiled=True),
        lax.all_gather(value_low, "ctx", axis=1, tiled=True),
    )
    query_groups = group_heads(query_rot, per_group)
    attended, log_total = lax.map(
        partial(attend_block, scaling=scaling),
        (query_groups, group_heads(keys_all, per_group), group_heads(values_all, per_group)),
    )
    attended_low = ungroup_heads(attended, seq_count).astype(jnp.bfloat16)
    branch_part = jnp.einsum(
        "ste,ed->std", attended_low, full_out, preferred_element_type=jnp.float32
    )
    middle = inputs_f + lax.psum(branch_part, "tp")
    second_out, normed_two, inverse_two = scaled_norm(
        middle, gains_f[1], modulation[:, 2], modulation[:, 3]
    )
    second_low = second_out.astype(jnp.bfloat16)
    hidden = jnp.einsum("std,df->stf", second_low, full_up, preferred_element_type=jnp.float32)
    activated = jax.nn.gelu(hidden, approximate=False).astype(jnp.bfloat16)
    mlp_part = jnp.einsum("stf,fd->std", activated, full_down, preferred_element_type=jnp.float32)
    output = (middle + lax.psum(mlp_part, "tp")).astype(jnp.bfloat16)
    back_qkv, back_out, back_up, back_down = (
        lax.all_gather(qkv_weight, "shard", axis=1, tiled=True),
        lax.all_gather(out_weight, "shard", axis=1, tiled=True),
        lax.all_gather(up_weight, "shard", axis=0, tiled=True),
        lax.all_gather(down_weight, "shard", axis=1, tiled=True),
    )
    keys_back, values_back = (
        lax.all_gather(key_rot, "ctx", axis=1, tiled=True),
        lax.all_gather(value_low, "ctx", axis=1, tiled=True),
    )
    grad_down = jnp.einsum("stf,std->fd", activated, cotangent, preferred_element_type=jnp.float32)
    grad_act = jnp.einsum("std,fd->stf", cotangent, back_down, preferred_element_type=jnp.float32)
    grad_hidden = (grad_act * gelu_slope(hidden)).astype(jnp.bfloat16)
    grad_up = jnp.einsum("std,stf->df", second_low, grad_hidden, preferred_element_type=jnp.float32)
    grad_second = lax.psum(
        jnp.einsum("stf,df->std", grad_hidden, back_up, preferred_element_type=jnp.float32), "tp"
    )
    grad_mid_norm, gain_two, scaling_two, offset_two = norm_back(
        grad_second, normed_two, inverse_two, gains_f[1], modulation[:, 2]
    )
    grad_middle = cotangent.astype(jnp.float32) + grad_mid_norm
    grad_branch = grad_middle.astype(jnp.bfloat16)
    grad_out = jnp.einsum(
        "ste,std->ed", attended_low, grad_branch, preferred_element_type=jnp.float32
    )
    grad_attended = jnp.einsum(
        "std,ed->ste", grad_branch, back_out, preferred_element_type=jnp.float32
    ).astype(jnp.bfloat16)
    grad_query_g, grad_key_g, grad_value_g = lax.map(
        partial(attend_back, scaling=scaling),
        (
            query_groups,
            group_heads(keys_back, per_group),
            group_heads(values_back, per_group),
            group_heads(grad_attended, per_group),
            log_total,
        ),
    )
    grad_key_all = ungroup_heads(grad_key_g, seq_count)
    grad_value_all = ungroup_heads(grad_value_g, seq_count)
    grad_key, grad_value = (
        lax.psum_scatter(grad_key_all, "ctx", scatter_dimension=1, tiled=True),
        lax.psum_scatter(grad_value_all, "ctx", scatter_dimension=1, tiled=True),
    )
    grad_query = ungroup_heads(grad_query_g, seq_count)
    query_back = unrotate(grad_query.reshape(head_shape), cosines, sines).reshape(
        seq_count, tokens, local_width
    )
    key_back = unrotate(grad_key.reshape(head_shape), cosines, sines).reshape(
        seq_count, tokens, local_width
    )
    grad_projected = jnp.stack([query_back, key_back, grad_value], axis=0).astype(jnp.bfloat16)
    grad_qkv = jnp.einsum(
        "std,cste->cde", first_low, grad_projected, preferred_element_type=jnp.float32
    )
    grad_first = lax.psum(
        jnp.einsum("cste,cde->std", grad_projected, back_qkv, preferred_element_type=jnp.float32),
        "tp",
    )
    grad_in_norm, gain_one, scaling_one, offset_one = norm_back(
        grad_first, normed_one, inverse_one, gains_f[0], modulation[:, 0]
    )
    input_grad = (grad_middle + grad_in_norm).astype(jnp.bfloat16)
    grad_modulation = jnp.stack([scaling_one, offset_one, scaling_two, offset_two], axis=1)
    grad_time = jnp.einsum("sk,scd->kcd", embedding, grad_modulation, precision=highest)
    grad_gains = jnp.stack([gain_one, gain_two], axis=0)
    shares = (
        lax.psum_scatter(grad_qkv, "shard", scatter_dimension=1, tiled=True),
        lax.psum_scatter(grad_out, "shard", scatter_dimension=1, tiled=True),
        lax.psum_scatter(grad_up, "shard", scatter_dimension=0, tiled=True),
        lax.psum_scatter(grad_down, "shard", scatter_dimension=1, tiled=True),
        lax.psum_scatter(grad_time, "shard", scatter_dimension=2, tiled=True),
        lax.psum_scatter(grad_gains, "shard", scatter_dimension=1, tiled=True),
    )
    shares = lax.psum((shares[0], shares[1], shares[2], shares[3], shares[4], shares[5]), "ctx")
    return (output, input_grad, shares[0], shares[1], shares[2], shares[3], shares[4], shares[5])


def solution(mesh):
    placed = (
        P("shard", "ctx", None),
        P("shard"),
        P("shard", "ctx"),
        P(None, "shard", "tp"),
        P("tp", "shard"),
        P("shard", "tp"),
        P("tp", "shard"),
        P(None, None, "shard"),
        P(None, "shard"),
        P("shard", "ctx", None),
    )
    return jax.shard_map(
        body,
        mesh=mesh,
        in_specs=placed,
        out_specs=(
            P("shard", "ctx", None),
            P("shard", "ctx", None),
            P(None, "shard", "tp"),
            P("tp", "shard"),
            P("shard", "tp"),
            P("tp", "shard"),
            P(None, None, "shard"),
            P(None, "shard"),
        ),
        check_vma=False,
    )
```

profile of v0, /device:TPU:0, one launch (start us, length us, event | category | flops | bytes accessed | tf_op | source)
XLA Modules:
  0.0 1433.2 jit_solution(13286509616975945891)
XLA Ops:
  11.3 9.6 all_gather.30
  24.3 23.4 %all-gather.8.cloned.1.call-done = bf16[256,4,1024]{2,1,0:T(4,128)(2,1)} async-done(((bf16[256,4,256]{2,1,0:T(4,128)(2,1)}), bf16[256,4,1024]{2,1,0:T(4,128)(2,1)}) %all-gather.8.cloned.1.call-update) | async-done | bytes 2097168 | tf_op jit(solution)/shard_map/all_gather | solution.py:150
  51.8 29.2 %all-gather.10.cloned.1.call-done = bf16[3,1024,256]{1,2,0:T(8,128)(2,1)} async-done(((bf16[3,256,256]{1,2,0:T(8,128)(2,1)}), bf16[3,1024,256]{1,2,0:T(8,128)(2,1)}) %all-gather.10.cloned.1.call-update) | async-done | bytes 1572880 | tf_op jit(solution)/shard_map/all_gather | solution.py:146
  88.6 14.1 all_gather.35
  111.5 35.0 %while.28 = (s32[]{:T(128)}, bf16[4,1,1024,64]{2,3,1,0:T(8,128)(2,1)}, f32[4,1,1024]{2,1,0:T(1,128)S(1)}, bf16[4,1,1024,64]{3,2,1,0:T(8,128)(2,1)S(1)}, bf16[4,1...) while((s32[]{:T(128)}, bf16[4,1,1024,64]{2,3,1,0:T(8,128)(2,1)}, ...), condition=%wide.region_5.6_spmd.clone, body=%wide.region_2.5_spmd.sunk.clone | while | flops 555744256 | bytes 30976136 | solution.py:182
  151.9 153.9 %all-reduce.7.cloned.1.call-done = f32[1,1024,1024]{2,1,0:T(8,128)} async-done(((f32[1,1024,1024]{2,1,0:T(8,128)}), f32[1,1024,1024]{2,1,0:T(8,128)}) %all-reduce.7.cloned.1.call-update) | async-done | bytes 4194320 | tf_op jit(solution)/shard_map/psum | solution.py:190
  311.0 31.0 %all-gather.14.cloned.1.call-done = bf16[1024,1024]{1,0:T(8,128)(2,1)} async-done(((bf16[256,1024]{1,0:T(8,128)(2,1)}), bf16[1024,1024]{1,0:T(8,128)(2,1)}) %all-gather.14.cloned.1.call-update) | async-done | bytes 2097168 | tf_op jit(solution)/shard_map/all_gather | solution.py:148
  342.0 15.0 %fusion.66 = (bf16[1024,1024]{1,0:T(8,128)(2,1)}, f32[1024,1024]{1,0:T(8,128)}) fusion(bf16[1024,1024]{1,0:T(8,128)(2,1)} %all-gather.14.cloned.1.call-done, f32[1,1024,1024]{2,1,0:T(8,128)} %copy-done, f32[1024]{0:T(1024)S(1)} %bitcast.301, f32[1024]{0:T(1024)S(1)} %bitcast.283, f32[1024]{0:T(1024)S(1)} %bitcast.279, f32[1024]{0:T(1024)S(1)} %add_rsqrt_fusion, ...), kind=kOutput, calls=%fused_computation.77 | convolution fusion | flops 2221932544 | bytes 12603392 | tf_op jit(solution)/shard_map/std,df->stf/dot_general | solution.py:195
  356.9 22.2 %all-gather.16.cloned.1.call-done = bf16[1024,1024]{1,0:T(8,128)(2,1)} async-done(((bf16[1024,256]{1,0:T(8,128)(2,1)}), bf16[1024,1024]{1,0:T(8,128)(2,1)}) %all-gather.16.cloned.1.call-update) | async-done | bytes 2097168 | tf_op jit(solution)/shard_map/all_gather | solution.py:149
  391.3 154.9 %all-reduce.9.cloned.1.call-done = f32[1,1024,1024]{2,1,0:T(8,128)} async-done(((f32[1,1024,1024]{2,1,0:T(8,128)}), f32[1,1024,1024]{2,1,0:T(8,128)}) %all-reduce.9.cloned.1.call-update) | async-done | bytes 4194320 | tf_op jit(solution)/shard_map/psum | solution.py:213
  560.0 51.6 %while.29 = (s32[]{:T(128)}, f32[4,1,1024,64]{2,3,1,0:T(8,128)}, f32[4,1,2048,64]{2,3,1,0:T(8,128)}, f32[4,1,2048,64]{2,3,1,0:T(8,128)}, bf16[4,1,1024,64]{3,2,1...) while((s32[]{:T(128)}, f32[4,1,1024,64]{2,3,1,0:T(8,128)}, ...), condition=%wide.region_15.16_spmd.clone, body=%wide.region_13.15_spmd.sunk.clone | while | flops 1367538688 | bytes 68977792 | solution.py:227
  624.5 9.5 reduce-scatter.15.cloned.1.call-done
  641.2 292.3 %all-reduce.11.cloned.1.call-done = (f32[1,1024,1024]{2,1,0:T(8,128)}, f32[1,1024,1024]{2,1,0:T(8,128)}) async-done(((f32[1,1024,1024]{2,1,0:T(8,128)}, f32[1,1024,1024]{2,1,0:T(8,128)}), (f32[1,1024,1024]{2,1,0:T(8,128)}, f32[1,1024,1024]{2,1,0:T(8,128)})) %all-reduce.11.cloned.1.call-update) | async-done | bytes 8388624 | tf_op jit(solution)/shard_map/psum | solution.py:198
  940.3 64.8 %copy.59 = f32[256,4,1024]{1,0,2:T(8,128)} copy(f32[256,4,1024]{2,1,0:T(4,128)} %broadcast_multiply_fusion) | data formatting | bytes 8388608
  1005.1 110.5 %reshape.619 = f32[1024,1024]{1,0:T(8,128)} reshape(f32[1024,256,4]{2,1,0:T(8,128)} %bitcast.86) | data formatting | bytes 8388608
  1128.5 7.7 fusion.106
  1143.3 24.2 %reduce-scatter.25.cloned.1.call-done = f32[256,1024]{1,0:T(8,128)} async-done(((f32[1024,1024]{1,0:T(8,128)}), f32[256,1024]{1,0:T(8,128)}) %reduce-scatter.25.cloned.1.call-update) | async-done | bytes 1048592
  1167.5 36.8 %reshape.620 = f32[256,256,4]{2,1,0:T(8,128)} reshape(f32[256,1024]{1,0:T(8,128)} %reduce-scatter.25.cloned.1.call-done) | data formatting | bytes 2097152
  1204.3 21.0 %copy.60 = f32[256,4,256]{2,1,0:T(4,128)} copy(f32[256,4,256]{1,0,2:T(8,128)} %bitcast.252) | data formatting | bytes 2097152
  1225.3 29.1 %reduce-scatter.23.cloned.1.call-done = f32[1024,256]{1,0:T(8,128)} async-done(((f32[1024,1024]{1,0:T(8,128)}), f32[1024,256]{1,0:T(8,128)}) %reduce-scatter.23.cloned.1.call-update) | async-done | bytes 1048592 | tf_op jit(solution)/shard_map/reduce_scatter | solution.py:269
  1254.5 55.8 %reduce-scatter.21.cloned.1.call-done = f32[256,1024]{1,0:T(8,128)} async-done(((f32[1024,1024]{1,0:T(8,128)}), f32[256,1024]{1,0:T(8,128)}) %reduce-scatter.21.cloned.1.call-update) | async-done | bytes 1048592 | tf_op jit(solution)/shard_map/reduce_scatter | solution.py:268
  1310.3 46.8 %reduce-scatter.17.cloned.1.call-done = f32[3,256,256]{1,2,0:T(8,128)} async-done(((f32[3,1024,256]{1,2,0:T(8,128)}), f32[3,256,256]{1,2,0:T(8,128)}) %reduce-scatter.17.cloned.1.call-update) | async-done | bytes 786448 | tf_op jit(solution)/shard_map/reduce_scatter | solution.py:266
  1366.4 18.8 %reduce-scatter.27.cloned.1.call-done = f32[256,2]{1,0:T(8,128)} async-done(((f32[1024,2]{1,0:T(8,128)}), f32[256,2]{1,0:T(8,128)}) %reduce-scatter.27.cloned.1.call-update) | async-done | bytes 2064
  1389.2 28.7 %all-reduce.13.cloned.1.call-done = (f32[3,256,256]{1,2,0:T(8,128)}, f32[256,256]{1,0:T(8,128)}, f32[256,1024]{1,0:T(8,128)}, f32[1024,256]{1,0:T(8,128)}, f32[256,4,256]{2,1,0:T(4,128)}) async-done(((f32[3,256,256]{1,2,0:T(8,128)}, f32[256,256]{1,0:T(8,128)}, f32[256,1024]{1,0:T(8,128)}, f32[1024,256]{1,0:T(8,128)}, f32[256,4,256]{2,1,0:T(4,128)}), (f32[3,256,256]{1,2,0:T(8,128)}, f32[256,256]{1,0:T(8,128)}, ...) | async-done | bytes 4194320 | tf_op jit(solution)/shard_map/psum | solution.py:273
  (286 shorter events, 217.9 us)
Async XLA Ops:
  7.2 40.6 %all-gather.8.cloned.1.call-start = ((), (), s32[]{:S(2)}) async-start(), calls=%async_computation.8 | async-start | bytes 2621440 | tf_op jit(solution)/shard_map/all_gather | solution.py:150
  7.9 73.1 %all-gather.10.cloned.1.call-start = ((), (), s32[]{:S(2)}) async-start(), calls=%async_computation.9 | async-start | bytes 1966080 | tf_op jit(solution)/shard_map/all_gather | solution.py:146
  9.9 96.0 %all-gather.12.cloned.1.call-start = ((), (), s32[]{:S(2)}) async-start(), calls=%async_computation.10 | async-start | bytes 1572864 | tf_op jit(solution)/shard_map/all_gather | solution.py:178
  23.8 522.3 %copy-start.36 = (f32[1,1024]{1,0:T(1,128)}, f32[1,1024]{1,0:T(1,128)S(1)}, u32[]{:S(2)}) copy-start(f32[1,1024]{1,0:T(1,128)S(1)} %get-tuple-element.239) | copy-start | bytes 12292
  51.8 494.3 %copy-start.39 = (f32[1,1,1024]{2,1,0:T(1,128)}, f32[1,1,1024]{2,1,0:T(1,128)S(1)}, u32[]{:S(2)}) copy-start(f32[1,1,1024]{2,1,0:T(1,128)S(1)} %get-tuple-element.233) | copy-start | bytes 12292
  86.3 22.4 %all-gather.18.cloned.1.call-start = ((), (), s32[]{:S(2)}) async-start(), calls=%async_computation.21 | async-start | bytes 1572864 | tf_op jit(solution)/shard_map/all_gather | solution.py:179
  88.5 217.2 %all-reduce.7.cloned.1.call-start = ((), (), s32[]{:S(2)}) async-start(), calls=%async_computation.11 | async-start | bytes 8388608 | tf_op jit(solution)/shard_map/psum | solution.py:190
  150.5 191.5 %all-gather.14.cloned.1.call-start = ((), (), s32[]{:S(2)}) async-start(), calls=%async_computation.12 | async-start | bytes 2621440 | tf_op jit(solution)/shard_map/all_gather | solution.py:148
  151.1 228.0 %all-gather.16.cloned.1.call-start = ((), (), s32[]{:S(2)}) async-start(), calls=%async_computation.13 | async-start | bytes 2621440 | tf_op jit(solution)/shard_map/all_gather | solution.py:149
  151.8 394.3 %all-reduce.9.cloned.1.call-start = ((), (), s32[]{:S(2)}) async-start(), calls=%async_computation.14 | async-start | bytes 8388608 | tf_op jit(solution)/shard_map/psum | solution.py:213
  391.0 231.4 %reduce-scatter.13.cloned.1.call-start = ((), (), s32[]{:S(2)}) async-start(), calls=%async_computation.15 | async-start | bytes 3145728 | tf_op jit(solution)/shard_map/reduce_scatter | solution.py:240
  611.6 22.4 %reduce-scatter.15.cloned.1.call-start = ((), (), s32[]{:S(2)}) async-start(), calls=%async_computation.16 | async-start | bytes 3145728 | tf_op jit(solution)/shard_map/reduce_scatter | solution.py:241
  614.6 318.9 %all-reduce.11.cloned.1.call-start = ((), (), s32[]{:S(2)}) async-start(), calls=%async_computation.24 | async-start | bytes 16777216 | tf_op jit(solution)/shard_map/psum | solution.py:198
  640.5 292.9 %copy-start.5 = (bf16[1,1024,1024]{2,1,0:T(8,128)(2,1)S(1)}, bf16[1,1024,1024]{2,1,0:T(8,128)(2,1)}, u32[]{:S(2)}) copy-start(bf16[1,1024,1024]{2,1,0:T(8,128)(2,1)} %param.14) | copy-start | bytes 6291460
  640.5 292.9 %copy-start.30 = (f32[1024]{0:T(1024)S(1)}, f32[1024]{0:T(1024)}, u32[]{:S(2)}) copy-start(f32[1024]{0:T(1024)} %copy-done.29) | copy-start | bytes 12292
  640.5 292.9 %copy-start.34 = (f32[1024]{0:T(1024)S(1)}, f32[1024]{0:T(1024)}, u32[]{:S(2)}) copy-start(f32[1024]{0:T(1024)} %copy-done.33) | copy-start | bytes 12292
  640.5 292.9 %copy-start.35 = (f32[1,1,1024]{2,1,0:T(1,128)S(1)}, f32[1,1,1024]{2,1,0:T(1,128)}, u32[]{:S(2)}) copy-start(f32[1,1,1024]{2,1,0:T(1,128)} %get-tuple-element.231) | copy-start | bytes 12292
  640.6 526.9 %reduce-scatter.25.cloned.1.call-start = ((), (), s32[]{:S(2)}) async-start(), calls=%async_computation.22 | async-start | bytes 5242880
  1115.6 109.7 %reduce-scatter.19.cloned.1.call-start = ((), (), s32[]{:S(2)}) async-start(), calls=%async_computation.18 | async-start | bytes 1310720 | tf_op jit(solution)/shard_map/reduce_scatter | solution.py:267
  1120.5 134.0 %reduce-scatter.23.cloned.1.call-start = ((), (), s32[]{:S(2)}) async-start(), calls=%async_computation.20 | async-start | bytes 5242880 | tf_op jit(solution)/shard_map/reduce_scatter | solution.py:269
  1127.9 182.4 %reduce-scatter.21.cloned.1.call-start = ((), (), s32[]{:S(2)}) async-start(), calls=%async_computation.19 | async-start | bytes 5242880 | tf_op jit(solution)/shard_map/reduce_scatter | solution.py:268
  1136.3 220.8 %reduce-scatter.17.cloned.1.call-start = ((), (), s32[]{:S(2)}) async-start(), calls=%async_computation.17 | async-start | bytes 3932160 | tf_op jit(solution)/shard_map/reduce_scatter | solution.py:266
  1142.1 243.0 %reduce-scatter.27.cloned.1.call-start = ((), (), s32[]{:S(2)}) async-start(), calls=%async_computation.23 | async-start | bytes 655360
  1143.3 274.5 %all-reduce.13.cloned.1.call-start = ((), (), s32[]{:S(2)}) async-start(), calls=%async_computation.25 | async-start | bytes 8388608 | tf_op jit(solution)/shard_map/psum | solution.py:273
  (58 other events, 1990.5 us)
Sparse Core Ops, SparseCore 0:
  9.8 37.8 all-gather.7
  50.1 30.8 all-gather.9
  86.5 9.0 all-gather.11
  97.5 10.1 all-gather.17
  150.6 155.0 all-reduce.6
  307.6 34.3 all-gather.13
  343.9 35.1 all-gather.15
  391.1 154.9 all-reduce.8
  611.7 8.5 reduce-scatter.12
  623.1 10.8 reduce-scatter.14
  640.7 292.6 all-reduce.10
  1115.7 51.7 reduce-scatter.24
  1171.2 27.6 reduce-scatter.18
  1201.8 52.6 reduce-scatter.22
  1257.6 52.6 reduce-scatter.20
  1313.1 43.9 reduce-scatter.16
  1360.4 24.7 reduce-scatter.26
  1388.8 28.9 all-reduce.12
where the time goes:
time: 1440 us; the launch traced here: 1430 us
  waiting for transfers between devices  922 us (64%)
  local copies, waits for them, and re-layouts  273 us (19%)
  matrix products  141 us (10%)
  other arithmetic  53.4 us (4%)
  blocking collectives  26.7 us (2%)
  between operations  15.8 us (1%)
    psum x1, waiting for transfers between devices, body(): output = (middle + lax.psum(mlp_part, 'tp')).astype(jnp.bfloat16)  292 us
    unnamed x116, local copies, waits for them, and re-layouts  255 us
    psum x1, waiting for transfers between devices, body(): lax.psum(jnp.einsum('stf,df->std', grad_hidden, back_up, preferred_elemen...  155 us
    psum x1, waiting for transfers between devices, body(): middle = inputs_f + lax.psum(branch_part, 'tp')  154 us
    reduce_scatter x1, waiting for transfers between devices, body(): lax.psum_scatter(grad_up, 'shard', scatter_dimension=0, tiled=True)  55.8 us
    reduce_scatter x1, waiting for transfers between devices, body(): lax.psum_scatter(grad_qkv, 'shard', scatter_dimension=1, tiled=True)  46.8 us
    unnamed x20, waiting for transfers between devices  44.9 us
    all_gather x1, waiting for transfers between devices, body(): lax.all_gather(up_weight, 'shard', axis=0, tiled=True)  31 us
  transfers between devices with their start and end apart: 18, of which 14 were waited for; matrix products, arithmetic and copies ran while one was open for 10% of the time, Pallas kernels for 0%

commit v1 on v0

--- a/solution.py
+++ b/solution.py
@@ -9,6 +9,13 @@
 TEMB = 256
 highest = lax.Precision.HIGHEST
 norm_epsilon = 1e-05
+
+
+def exchange_gather(value, axis, dim):
+    devices = lax.axis_size(axis)
+    shards = jnp.stack([value for _ in range(devices)])
+    shards = lax.all_to_all(shards, axis, split_axis=0, concat_axis=0)
+    return jnp.concatenate(shards, axis=dim)
 
 
 def embed_time(timestep):
@@ -145,7 +152,7 @@
     full_qkv, full_out, full_up, full_down, full_time, full_gains = (
         lax.all_gather(qkv_weight, "shard", axis=1, tiled=True),
         lax.all_gather(out_weight, "shard", axis=1, tiled=True),
-        lax.all_gather(up_weight, "shard", axis=0, tiled=True),
+        exchange_gather(up_weight, "shard", 0),
         lax.all_gather(down_weight, "shard", axis=1, tiled=True),
         lax.all_gather(time_weight, "shard", axis=2, tiled=True),
         lax.all_gather(norm_gains, "shard", axis=1, tiled=True),

time: 1440 us -> 1440 us (level)
    unnamed x116 -> x112, local copies, waits for them, and re-layouts: 255 us -> 253 us
  transfers between devices with their start and end apart: 18 -> 19, of which waited for: 14 -> 14; matrix products, arithmetic and copies ran while one was open for 10% -> 10% of each run, Pallas kernels for 0% -> 0%
where the time goes in v1:
time: 1440 us; the launch traced here: 1430 us
  waiting for transfers between devices  908 us (63%)
  local copies, waits for them, and re-layouts  274 us (19%)
  matrix products  144 us (10%)
  other arithmetic  53.4 us (4%)
  blocking collectives  26.7 us (2%)
  between operations  15.8 us (1%)
    psum x1, waiting for transfers between devices, body(): output = (middle + lax.psum(mlp_part, 'tp')).astype(jnp.bfloat16)  292 us
    unnamed x112, local copies, waits for them, and re-layouts  253 us
    psum x1, waiting for transfers between devices, body(): lax.psum(jnp.einsum('stf,df->std', grad_hidden, back_up, preferred_elemen...  155 us
    psum x1, waiting for transfers between devices, body(): middle = inputs_f + lax.psum(branch_part, 'tp')  147 us
    reduce_scatter x1, waiting for transfers between devices, body(): lax.psum_scatter(grad_up, 'shard', scatter_dimension=0, tiled=True)  55.8 us
    reduce_scatter x1, waiting for transfers between devices, body(): lax.psum_scatter(grad_qkv, 'shard', scatter_dimension=1, tiled=True)  46.8 us
    unnamed x20, waiting for transfers between devices  44.9 us
    all_gather x1, waiting for transfers between devices, body(): lax.all_gather(up_weight, 'shard', axis=0, tiled=True)  30.6 us
  transfers between devices with their start and end apart: 19, of which 14 were waited for; matrix products, arithmetic and copies ran while one was open for 10% of the time, Pallas kernels for 0%

profile of v1, /device:TPU:0, one launch (start us, length us, event | category | flops | bytes accessed | tf_op | source)
XLA Modules:
  0.0 1428.0 jit_solution(17315601764469859636)
XLA Ops:
  11.3 9.6 all_gather.29
  24.3 23.4 %all-gather.8.cloned.1.call-done = bf16[256,4,1024]{2,1,0:T(4,128)(2,1)} async-done(((bf16[256,4,256]{2,1,0:T(4,128)(2,1)}), bf16[256,4,1024]{2,1,0:T(4,128)(2,1)}) %all-gather.8.cloned.1.call-update) | async-done | bytes 2097168 | tf_op jit(solution)/shard_map/all_gather | solution.py:157
  51.8 29.2 %all-gather.10.cloned.1.call-done = bf16[3,1024,256]{1,2,0:T(8,128)(2,1)} async-done(((bf16[3,256,256]{1,2,0:T(8,128)(2,1)}), bf16[3,1024,256]{1,2,0:T(8,128)(2,1)}) %all-gather.10.cloned.1.call-update) | async-done | bytes 1572880 | tf_op jit(solution)/shard_map/all_gather | solution.py:153
  88.6 14.1 all_gather.34
  111.5 35.0 %while.28 = (s32[]{:T(128)}, bf16[4,1,1024,64]{2,3,1,0:T(8,128)(2,1)}, f32[4,1,1024]{2,1,0:T(1,128)S(1)}, bf16[4,1,1024,64]{3,2,1,0:T(8,128)(2,1)S(1)}, bf16[4,1...) while((s32[]{:T(128)}, bf16[4,1,1024,64]{2,3,1,0:T(8,128)(2,1)}, ...), condition=%wide.region_5.6_spmd.clone, body=%wide.region_2.5_spmd.sunk.clone | while | flops 555744256 | bytes 30976136 | solution.py:189
  159.2 146.6 %all-reduce.7.cloned.1.call-done = f32[1,1024,1024]{2,1,0:T(8,128)} async-done(((f32[1,1024,1024]{2,1,0:T(8,128)}), f32[1,1024,1024]{2,1,0:T(8,128)}) %all-reduce.7.cloned.1.call-update) | async-done | bytes 4194320 | tf_op jit(solution)/shard_map/psum | solution.py:197
  311.0 15.0 %fusion.66 = (bf16[1024,1024]{1,0:T(8,128)(2,1)}, f32[1024,1024]{1,0:T(8,128)}) fusion(bf16[1024,1024]{1,0:T(8,128)(2,1)} %bitcast.47, f32[1,1024,1024]{2,1,0:T(8,128)} %copy-done, f32[1024]{0:T(1024)S(1)} %bitcast.302, f32[1024]{0:T(1024)S(1)} %bitcast.284, f32[1024]{0:T(1024)S(1)} %bitcast.280, f32[1024]{0:T(1024)S(1)} %add_rsqrt_fusion, ...), kind=kOutput, calls=%fused_computation.77 | convolution fusion | flops 2221932544 | bytes 12603392 | tf_op jit(solution)/shard_map/std,df->stf/dot_general | solution.py:202
  326.0 15.8 %all-gather.14.cloned.1.call-done = bf16[1024,1024]{1,0:T(8,128)(2,1)} async-done(((bf16[1024,256]{1,0:T(8,128)(2,1)}), bf16[1024,1024]{1,0:T(8,128)(2,1)}) %all-gather.14.cloned.1.call-update) | async-done | bytes 2097168 | tf_op jit(solution)/shard_map/all_gather | solution.py:156
  348.5 30.6 %all-gather.16.cloned.1.call-done = bf16[1024,1024]{1,0:T(8,128)(2,1)} async-done(((bf16[256,1024]{1,0:T(8,128)(2,1)}), bf16[1024,1024]{1,0:T(8,128)(2,1)}) %all-gather.16.cloned.1.call-update) | async-done | bytes 2097168 | tf_op jit(solution)/shard_map/all_gather | solution.py:209
  386.1 154.8 %all-reduce.9.cloned.1.call-done = f32[1,1024,1024]{2,1,0:T(8,128)} async-done(((f32[1,1024,1024]{2,1,0:T(8,128)}), f32[1,1024,1024]{2,1,0:T(8,128)}) %all-reduce.9.cloned.1.call-update) | async-done | bytes 4194320 | tf_op jit(solution)/shard_map/psum | solution.py:220
  554.8 51.6 %while.29 = (s32[]{:T(128)}, f32[4,1,1024,64]{2,3,1,0:T(8,128)}, f32[4,1,2048,64]{2,3,1,0:T(8,128)}, f32[4,1,2048,64]{2,3,1,0:T(8,128)}, bf16[4,1,1024,64]{3,2,1...) while((s32[]{:T(128)}, f32[4,1,1024,64]{2,3,1,0:T(8,128)}, ...), condition=%wide.region_15.16_spmd.clone, body=%wide.region_13.15_spmd.sunk.clone | while | flops 1367538688 | bytes 68977792 | solution.py:234
  619.3 9.5 reduce-scatter.15.cloned.1.call-done
  636.0 292.3 %all-reduce.11.cloned.1.call-done = (f32[1,1024,1024]{2,1,0:T(8,128)}, f32[1,1024,1024]{2,1,0:T(8,128)}) async-done(((f32[1,1024,1024]{2,1,0:T(8,128)}, f32[1,1024,1024]{2,1,0:T(8,128)}), (f32[1,1024,1024]{2,1,0:T(8,128)}, f32[1,1024,1024]{2,1,0:T(8,128)})) %all-reduce.11.cloned.1.call-update) | async-done | bytes 8388624 | tf_op jit(solution)/shard_map/psum | solution.py:205
  935.1 64.8 %copy.59 = f32[256,4,1024]{1,0,2:T(8,128)} copy(f32[256,4,1024]{2,1,0:T(4,128)} %broadcast_multiply_fusion) | data formatting | bytes 8388608
  999.9 110.5 %reshape.625 = f32[1024,1024]{1,0:T(8,128)} reshape(f32[1024,256,4]{2,1,0:T(8,128)} %bitcast.87) | data formatting | bytes 8388608
  1123.3 7.7 fusion.106
  1138.1 24.2 %reduce-scatter.25.cloned.1.call-done = f32[256,1024]{1,0:T(8,128)} async-done(((f32[1024,1024]{1,0:T(8,128)}), f32[256,1024]{1,0:T(8,128)}) %reduce-scatter.25.cloned.1.call-update) | async-done | bytes 1048592
  1162.3 36.8 %reshape.626 = f32[256,256,4]{2,1,0:T(8,128)} reshape(f32[256,1024]{1,0:T(8,128)} %reduce-scatter.25.cloned.1.call-done) | data formatting | bytes 2097152
  1199.1 21.0 %copy.60 = f32[256,4,256]{2,1,0:T(4,128)} copy(f32[256,4,256]{1,0,2:T(8,128)} %bitcast.253) | data formatting | bytes 2097152
  1220.1 29.1 %reduce-scatter.23.cloned.1.call-done = f32[1024,256]{1,0:T(8,128)} async-done(((f32[1024,1024]{1,0:T(8,128)}), f32[1024,256]{1,0:T(8,128)}) %reduce-scatter.23.cloned.1.call-update) | async-done | bytes 1048592 | tf_op jit(solution)/shard_map/reduce_scatter | solution.py:276
  1249.3 55.8 %reduce-scatter.21.cloned.1.call-done = f32[256,1024]{1,0:T(8,128)} async-done(((f32[1024,1024]{1,0:T(8,128)}), f32[256,1024]{1,0:T(8,128)}) %reduce-scatter.21.cloned.1.call-update) | async-done | bytes 1048592 | tf_op jit(solution)/shard_map/reduce_scatter | solution.py:275
  1305.1 46.8 %reduce-scatter.17.cloned.1.call-done = f32[3,256,256]{1,2,0:T(8,128)} async-done(((f32[3,1024,256]{1,2,0:T(8,128)}), f32[3,256,256]{1,2,0:T(8,128)}) %reduce-scatter.17.cloned.1.call-update) | async-done | bytes 786448 | tf_op jit(solution)/shard_map/reduce_scatter | solution.py:273
  1361.2 18.8 %reduce-scatter.27.cloned.1.call-done = f32[256,2]{1,0:T(8,128)} async-done(((f32[1024,2]{1,0:T(8,128)}), f32[256,2]{1,0:T(8,128)}) %reduce-scatter.27.cloned.1.call-update) | async-done | bytes 2064
  1383.9 28.7 %all-reduce.13.cloned.1.call-done = (f32[3,256,256]{1,2,0:T(8,128)}, f32[256,256]{1,0:T(8,128)}, f32[256,1024]{1,0:T(8,128)}, f32[1024,256]{1,0:T(8,128)}, f32[256,4,256]{2,1,0:T(4,128)}) async-done(((f32[3,256,256]{1,2,0:T(8,128)}, f32[256,256]{1,0:T(8,128)}, f32[256,1024]{1,0:T(8,128)}, f32[1024,256]{1,0:T(8,128)}, f32[256,4,256]{2,1,0:T(4,128)}), (f32[3,256,256]{1,2,0:T(8,128)}, f32[256,256]{1,0:T(8,128)}, ...) | async-done | bytes 4194320 | tf_op jit(solution)/shard_map/psum | solution.py:280
  (285 shorter events, 226.8 us)
Async XLA Ops:
  7.2 40.6 %all-gather.8.cloned.1.call-start = ((), (), s32[]{:S(2)}) async-start(), calls=%async_computation.9 | async-start | bytes 2621440 | tf_op jit(solution)/shard_map/all_gather | solution.py:157
  7.9 73.1 %all-gather.10.cloned.1.call-start = ((), (), s32[]{:S(2)}) async-start(), calls=%async_computation.10 | async-start | bytes 1966080 | tf_op jit(solution)/shard_map/all_gather | solution.py:153
  9.9 96.0 %all-gather.12.cloned.1.call-start = ((), (), s32[]{:S(2)}) async-start(), calls=%async_computation.11 | async-start | bytes 1572864 | tf_op jit(solution)/shard_map/all_gather | solution.py:185
  23.8 517.1 %copy-start.36 = (f32[1,1024]{1,0:T(1,128)}, f32[1,1024]{1,0:T(1,128)S(1)}, u32[]{:S(2)}) copy-start(f32[1,1024]{1,0:T(1,128)S(1)} %get-tuple-element.239) | copy-start | bytes 12292
  51.8 489.1 %copy-start.39 = (f32[1,1,1024]{2,1,0:T(1,128)}, f32[1,1,1024]{2,1,0:T(1,128)S(1)}, u32[]{:S(2)}) copy-start(f32[1,1,1024]{2,1,0:T(1,128)S(1)} %get-tuple-element.233) | copy-start | bytes 12292
  86.3 22.4 %all-gather.18.cloned.1.call-start = ((), (), s32[]{:S(2)}) async-start(), calls=%async_computation.22 | async-start | bytes 1572864 | tf_op jit(solution)/shard_map/all_gather | solution.py:186
  88.5 217.2 %all-reduce.7.cloned.1.call-start = ((), (), s32[]{:S(2)}) async-start(), calls=%async_computation.12 | async-start | bytes 8388608 | tf_op jit(solution)/shard_map/psum | solution.py:197
  150.5 191.3 %all-gather.14.cloned.1.call-start = ((), (), s32[]{:S(2)}) async-start(), calls=%async_computation.13 | async-start | bytes 2621440 | tf_op jit(solution)/shard_map/all_gather | solution.py:156
  153.8 157.2 %all-to-all-start = ((bf16[4,256,1024]{2,1,0:T(8,128)(2,1)}), bf16[4,256,1024]{2,1,0:T(8,128)(2,1)}, u32[]{:S(2)}, u32[]{:S(2)}) async-start(bf16[4,256,1024]{2,1,0:T(8,128)(2,1)} %stack.39), calls=%async_computation | async-start | bytes 4194304 | tf_op jit(solution)/shard_map/all_to_all | solution.py:17
  158.4 220.8 %all-gather.16.cloned.1.call-start = ((), (), s32[]{:S(2)}) async-start(), calls=%async_computation.14 | async-start | bytes 2621440 | tf_op jit(solution)/shard_map/all_gather | solution.py:209
  159.1 381.8 %all-reduce.9.cloned.1.call-start = ((), (), s32[]{:S(2)}) async-start(), calls=%async_computation.15 | async-start | bytes 8388608 | tf_op jit(solution)/shard_map/psum | solution.py:220
  385.8 231.4 %reduce-scatter.13.cloned.1.call-start = ((), (), s32[]{:S(2)}) async-start(), calls=%async_computation.16 | async-start | bytes 3145728 | tf_op jit(solution)/shard_map/reduce_scatter | solution.py:247
  606.4 22.4 %reduce-scatter.15.cloned.1.call-start = ((), (), s32[]{:S(2)}) async-start(), calls=%async_computation.17 | async-start | bytes 3145728 | tf_op jit(solution)/shard_map/reduce_scatter | solution.py:248
  609.4 318.9 %all-reduce.11.cloned.1.call-start = ((), (), s32[]{:S(2)}) async-start(), calls=%async_computation.25 | async-start | bytes 16777216 | tf_op jit(solution)/shard_map/psum | solution.py:205
  635.3 292.9 %copy-start.5 = (bf16[1,1024,1024]{2,1,0:T(8,128)(2,1)S(1)}, bf16[1,1024,1024]{2,1,0:T(8,128)(2,1)}, u32[]{:S(2)}) copy-start(bf16[1,1024,1024]{2,1,0:T(8,128)(2,1)} %param.14) | copy-start | bytes 6291460
  635.3 292.9 %copy-start.30 = (f32[1024]{0:T(1024)S(1)}, f32[1024]{0:T(1024)}, u32[]{:S(2)}) copy-start(f32[1024]{0:T(1024)} %copy-done.29) | copy-start | bytes 12292
  635.3 292.9 %copy-start.34 = (f32[1024]{0:T(1024)S(1)}, f32[1024]{0:T(1024)}, u32[]{:S(2)}) copy-start(f32[1024]{0:T(1024)} %copy-done.33) | copy-start | bytes 12292
  635.4 526.9 %reduce-scatter.25.cloned.1.call-start = ((), (), s32[]{:S(2)}) async-start(), calls=%async_computation.23 | async-start | bytes 5242880
  1110.4 109.7 %reduce-scatter.19.cloned.1.call-start = ((), (), s32[]{:S(2)}) async-start(), calls=%async_computation.19 | async-start | bytes 1310720 | tf_op jit(solution)/shard_map/reduce_scatter | solution.py:274
  1115.3 134.0 %reduce-scatter.23.cloned.1.call-start = ((), (), s32[]{:S(2)}) async-start(), calls=%async_computation.21 | async-start | bytes 5242880 | tf_op jit(solution)/shard_map/reduce_scatter | solution.py:276
  1122.7 182.4 %reduce-scatter.21.cloned.1.call-start = ((), (), s32[]{:S(2)}) async-start(), calls=%async_computation.20 | async-start | bytes 5242880 | tf_op jit(solution)/shard_map/reduce_scatter | solution.py:275
  1131.1 220.8 %reduce-scatter.17.cloned.1.call-start = ((), (), s32[]{:S(2)}) async-start(), calls=%async_computation.18 | async-start | bytes 3932160 | tf_op jit(solution)/shard_map/reduce_scatter | solution.py:273
  1136.9 243.0 %reduce-scatter.27.cloned.1.call-start = ((), (), s32[]{:S(2)}) async-start(), calls=%async_computation.24 | async-start | bytes 655360
  1138.1 274.5 %all-reduce.13.cloned.1.call-start = ((), (), s32[]{:S(2)}) async-start(), calls=%async_computation.26 | async-start | bytes 8388608 | tf_op jit(solution)/shard_map/psum | solution.py:280
  (57 other events, 2226.9 us)
Sparse Core Ops, SparseCore 0:
  9.8 37.8 all-gather.7
  50.1 30.8 all-gather.9
  86.5 9.0 all-gather.11
  97.5 10.1 all-gather.17
  150.6 155.0 all-reduce.6
  307.6 34.1 all-gather.13
  343.8 35.3 all-gather.15
  385.9 154.9 all-reduce.8
  606.5 8.5 reduce-scatter.12
  617.9 10.8 reduce-scatter.14
  635.5 292.6 all-reduce.10
  1110.5 51.7 reduce-scatter.24
  1166.0 27.6 reduce-scatter.18
  1196.6 52.6 reduce-scatter.22
  1252.4 52.6 reduce-scatter.20
  1307.9 43.9 reduce-scatter.16
  1355.2 24.7 reduce-scatter.26
  1383.6 28.9 all-reduce.12
